TPU v7x, 256 devices: a whole 4x4x8 slice. The times are simulated.
256 devices in a mesh: snap: 16 (over z, core), vert: 16 (over y, x).
Axes of the slice: x: 4, y: 4, z: 8, core: 2. Of those that a mesh axis runs over, the one named last changes fastest.
Arguments:
- saved_gates: bfloat16 [16, 8192, 1536], P(None, ('vert', 'snap')), may hold values from -1 to 1, as said below
- saved_cells: bfloat16 [16, 8192, 384], P(None, ('vert', 'snap')), may hold values from -4 to 4
- conv_out: float32 [16, 8192, 384], P(None, ('vert', 'snap')), may hold values from -6 to 6
- out_grad: float32 [16, 8192, 384], P(None, ('vert', 'snap')), may hold values from -6 to 6
- input_weight: float32 [384, 1536], replicated, may hold values from -0.3125 to 0.3125
- recur_weight: float32 [384, 1536], replicated, may hold values from -0.3125 to 0.3125
- conv_weight: float32 [384, 384], replicated, may hold values from -0.3125 to 0.3125
- node_feats: float32 [16, 8192, 384], P('snap', 'vert'), may hold values from -6 to 6
- tile_values: bfloat16 [16, 16, 5, 512, 512], P('snap', 'vert'), may hold values from -0.15625 to 0.15625
- tile_mask: int32 [16, 16, 5], P('snap', 'vert'), may hold values 0 or 1
Outputs:
- feat_grad: float32 [16, 8192, 384], P('snap', 'vert')
- conv_weight_grad: float32 [147456], P(('snap', 'vert'))
- input_weight_grad: float32 [589824], P(('snap', 'vert'))
- recur_weight_grad: float32 [589824], P(('snap', 'vert'))
Inputs may be any that keep to these rules, and one draw needn't show every extreme that they name: `saved_gates`: the first and fourth blocks of 384 entries lie strictly between 0 and 1, the second in (0, 1], the third strictly between -1 and 1.
All inputs are finite; a program needn't handle non-finite values. No bound on the sum of `tile_mask` on one device may be relied on, other than what follows from the above.
Results may differ from a plain program's by a relative error of at most 0.0029.
Values may be sent and summed in bfloat16 or wider, within the bound.
A program may use at most 128 MiB of HBM per device.

v0:
```python
import jax
import jax.numpy as jnp
from jax import lax
from jax.sharding import PartitionSpec as P


def passed_along(shard, axis, by):
    size = lax.axis_size(axis)
    pairs = [(i, i + by) for i in range(size) if 0 <= i + by < size]
    return lax.ppermute(shard, axis, pairs)


def cell_backward(saved_gates, saved_cells, out_grad, recur_weight):
    feat_width = saved_cells.shape[-1]
    gate_vals = saved_gates.astype(jnp.float32)
    cell_vals = saved_cells.astype(jnp.float32)
    prev_cells = jnp.concatenate([jnp.zeros_like(cell_vals[:1]), cell_vals[:-1]], axis=0)

    def reverse_step(carry, inputs):
        rec_grad, cell_grad = carry
        gate_now, cell_now, cell_before, grad_now = inputs
        in_gate = gate_now[:, :feat_width]
        forget = gate_now[:, feat_width : 2 * feat_width]
        candidate = gate_now[:, 2 * feat_width : 3 * feat_width]
        out_gate = gate_now[:, 3 * feat_width :]
        total_grad = grad_now + rec_grad
        squashed = jnp.tanh(cell_now)
        cell_total = cell_grad + total_grad * out_gate * (1.0 - squashed * squashed)
        pre_grad = jnp.concatenate(
            [
                cell_total * candidate * in_gate * (1.0 - in_gate),
                cell_total * cell_before * forget * (1.0 - forget),
                cell_total * in_gate * (1.0 - candidate * candidate),
                total_grad * squashed * out_gate * (1.0 - out_gate),
            ],
            axis=-1,
        )
        new_rec = jnp.dot(
            pre_grad,
            recur_weight.T,
            precision=lax.Precision.HIGHEST,
            preferred_element_type=jnp.float32,
        )
        return ((new_rec, cell_total * forget), pre_grad)

    row_total = cell_vals.shape[1]
    begin = (
        jnp.zeros((row_total, feat_width), jnp.float32),
        jnp.zeros((row_total, feat_width), jnp.float32),
    )
    unused, pre_grads = lax.scan(
        reverse_step, begin, (gate_vals, cell_vals, prev_cells, out_grad), reverse=True
    )
    last_out = gate_vals[:, :, 3 * feat_width :]
    prev_out = jnp.concatenate([jnp.zeros_like(last_out[:1]), last_out[:-1]], axis=0)
    prev_hidden = prev_out * jnp.tanh(prev_cells)
    return (pre_grads, prev_hidden)


def pass_direct(piece, offset):
    return passed_along(piece, "vert", offset)


def local(
    saved_gates,
    saved_cells,
    conv_out,
    out_grad,
    input_weight,
    recur_weight,
    conv_weight,
    node_feats,
    tile_values,
    tile_mask,
):
    pre_grads, prev_hidden = cell_backward(saved_gates, saved_cells, out_grad, recur_weight)
    conv_in_grad = jnp.einsum(
        "tvg,fg->tvf",
        pre_grads,
        input_weight,
        precision=lax.Precision.HIGHEST,
        preferred_element_type=jnp.float32,
    )
    input_term = jnp.einsum(
        "tvf,tvg->fg",
        conv_out,
        pre_grads,
        precision=lax.Precision.HIGHEST,
        preferred_element_type=jnp.float32,
    ).reshape(-1)
    recur_term = jnp.einsum(
        "tvf,tvg->fg",
        prev_hidden,
        pre_grads,
        precision=lax.Precision.HIGHEST,
        preferred_element_type=jnp.float32,
    ).reshape(-1)
    input_weight_grad, recur_weight_grad = (
        lax.psum_scatter(input_term, ("snap", "vert"), scatter_dimension=0, tiled=True),
        lax.psum_scatter(recur_term, ("snap", "vert"), scatter_dimension=0, tiled=True),
    )
    rounded = lax.all_to_all(
        conv_in_grad.astype(jnp.bfloat16), "snap", split_axis=0, concat_axis=1, tiled=True
    )
    tiles = tile_values[:, 0]
    partial_value = jnp.einsum("skij,sif->skjf", tiles, rounded, preferred_element_type=jnp.float32)
    slot_count = tiles.shape[1]
    reach_blocks = (slot_count - 1) // 2
    position = lax.axis_index("vert")
    block_count = lax.axis_size("vert")
    target = position + jnp.arange(slot_count, dtype=jnp.int32) - reach_blocks
    inside = (target >= 0) & (target < block_count)
    present = (tile_mask[:, 0, :] == 1) & inside[None, :]
    partial_value = partial_value * present.astype(jnp.float32)[:, :, None, None]
    z_grad = partial_value[:, reach_blocks]
    for slot in range(slot_count):
        offset = slot - reach_blocks
        if offset != 0:
            z_grad = z_grad + pass_direct(partial_value[:, slot], offset)
    feat_grad = jnp.einsum(
        "sbg,fg->sbf",
        z_grad,
        conv_weight,
        precision=lax.Precision.HIGHEST,
        preferred_element_type=jnp.float32,
    )
    conv_term = jnp.einsum(
        "sbf,sbg->fg",
        node_feats,
        z_grad,
        precision=lax.Precision.HIGHEST,
        preferred_element_type=jnp.float32,
    ).reshape(-1)
    conv_weight_grad = lax.psum_scatter(
        conv_term, ("snap", "vert"), scatter_dimension=0, tiled=True
    )
    return (feat_grad, conv_weight_grad, input_weight_grad, recur_weight_grad)


def solution(mesh):
    placed = (
        P(None, ("vert", "snap"), None),
        P(None, ("vert", "snap"), None),
        P(None, ("vert", "snap"), None),
        P(None, ("vert", "snap"), None),
        P(),
        P(),
        P(),
        P("snap", "vert", None),
        P("snap", "vert", None, None, None),
        P("snap", "vert", None),
    )
    return jax.shard_map(
        local,
        mesh=mesh,
        in_specs=placed,
        out_specs=(
            P("snap", "vert", None),
            P(("snap", "vert")),
            P(("snap", "vert")),
            P(("snap", "vert")),
        ),
        check_vma=False,
    )
```

profile of v0, /device:TPU:8, one launch (start us, length us, event | category | flops | bytes accessed | tf_op | source)
XLA Modules:
  0.0 538.3 jit_solution(3331778018956491245)
XLA Ops:
  7.2 1.2 slice.74
  8.4 2.0 convert_element_type.19
  10.4 3.5 convert_element_type.18
  14.8 2.1 broadcast_in_dim.15
  17.5 135.6 %while.19 = (s32[]{:T(128)}, f32[32,384]{1,0:T(8,128)}, f32[32,384]{1,0:T(8,128)}, f32[16,32,1536]{2,1,0:T(8,128)}, f32[16,32,384]{2,1,0:T(8,128)}, /*index=5*/f...) while((s32[]{:T(128)}, f32[32,384]{1,0:T(8,128)}, ...), condition=%wide.region_1.2_spmd.clone, body=%wide.region_0.1_spmd.clone.sunk | while | flops 227082240 | bytes 4227227 | solution.py:51
  18.4 1.5 slice_multiply_fusion.2
  21.5 4.5 fusion.44
  26.9 1.5 slice_multiply_fusion.2
  29.9 4.5 fusion.44
  35.4 1.5 slice_multiply_fusion.2
  38.4 4.5 fusion.44
  43.8 1.5 slice_multiply_fusion.2
  46.9 4.5 fusion.44
  52.3 1.5 slice_multiply_fusion.2
  55.3 4.5 fusion.44
  60.8 1.5 slice_multiply_fusion.2
  63.8 4.5 fusion.44
  69.2 1.5 slice_multiply_fusion.2
  72.3 4.5 fusion.44
  77.7 1.5 slice_multiply_fusion.2
  80.8 4.5 fusion.44
  86.2 1.5 slice_multiply_fusion.2
  89.3 4.5 fusion.44
  94.7 1.5 slice_multiply_fusion.2
  97.8 4.5 fusion.44
  103.2 1.5 slice_multiply_fusion.2
  106.2 4.5 fusion.44
  111.7 1.5 slice_multiply_fusion.2
  114.7 4.5 fusion.44
  120.2 1.5 slice_multiply_fusion.2
  123.2 4.5 fusion.44
  128.6 1.5 slice_multiply_fusion.2
  131.7 4.5 fusion.44
  137.1 1.5 slice_multiply_fusion.2
  140.2 4.5 fusion.44
  145.6 1.5 slice_multiply_fusion.2
  148.6 4.5 fusion.44
  153.1 8.5 %fusion.15 = bf16[16,32,384]{2,1,0:T(8,128)(2,1)} fusion(f32[16,32,1536]{2,1,0:T(8,128)} %get-tuple-element.183, f32[384,1536]{1,0:T(8,128)} %param.16), kind=kOutput, calls=%fused_computation.28 | convolution fusion | flops 3624075264 | bytes 5898240 | tf_op jit(solution)/shard_map/tvg,fg->tvf/dot_general | solution.py:77
  161.6 8.6 %all-to-all-start = ((bf16[16,32,384]{2,1,0:T(8,128)(2,1)}), bf16[16,32,384]{2,1,0:T(8,128)(2,1)}, u32[]{:S(2)}, u32[]{:S(2)}) async-start(bf16[16,32,384]{2,1,0:T(8,128)(2,1)} %fusion.15), calls=%async_computation | async-start | bytes 786432 | tf_op jit(solution)/shard_map/all_to_all | solution.py:102
  170.3 1.9 slice.80
  172.2 11.8 %all-to-all-done = bf16[16,32,384]{2,1,0:T(8,128)(2,1)} async-done(((bf16[16,32,384]{2,1,0:T(8,128)(2,1)}), bf16[16,32,384]{2,1,0:T(8,128)(2,1)}, u32[]{:S(2)}, u32[]{:S(2)}) %all-to-all-start) | async-done | bytes 393248 | tf_op jit(solution)/shard_map/all_to_all | solution.py:102
  184.0 2.2 multiply_bitcast_fusion
  186.2 1.7 slice_bitcast_fusion.3
  187.9 1.8 copy-done.1
  189.7 4.9 collective-permute-start
  194.6 3.1 collective-permute-start.1
  197.7 2.8 collective-permute-start.2
  200.5 2.6 collective-permute-start.3
  203.1 5.4 %convolution_bitcast_fusion = f32[384,1536]{1,0:T(8,128)} fusion(f32[16,32,1536]{2,1,0:T(8,128)S(1)} %copy-done.2, f32[15,32,384]{2,1,0:T(8,128)S(1)} %copy-done.4, f32[15,32,384]{2,1,0:T(8,128)S(1)} %slice.74), kind=kOutput, calls=%fused_computation.21 | convolution fusion | flops 3624075264 | bytes 6979584 | tf_op jit(solution)/shard_map/tvf,tvg->fg/dot_general | solution.py:91
  208.6 3.2 reshape.70
  211.8 7.7 %convolution_bitcast_fusion.1 = f32[384,1536]{0,1:T(8,128)} fusion(f32[16,32,1536]{2,1,0:T(8,128)} %get-tuple-element.183, f32[16,32,384]{2,1,0:T(8,128)S(1)} %copy-done.5), kind=kOutput, calls=%fused_computation.22 | convolution fusion | flops 3623878656 | bytes 6291456 | tf_op jit(solution)/shard_map/tvf,tvg->fg/dot_general | solution.py:84
  219.5 3.1 copy.20
  222.6 3.1 reshape.69
  225.8 4.8 collective-permute-done.1
  230.9 16.3 %collective-permute-done.3 = f32[1,512,384]{1,2,0:T(8,128)} collective-permute-done((f32[1,512,384]{1,2,0:T(8,128)}, f32[1,512,384]{1,2,0:T(8,128)}, u32[]{:S(2)}, u32[]{:S(2)}) %collective-permute-start.3) | collective-permute-done | bytes 786464 | tf_op jit(solution)/shard_map/ppermute | solution.py:10
  247.3 2.5 fusion.22
  249.8 2.2 convolution_bitcast_fusion.3
  252.0 2.1 copy.19
  254.2 1.9 reshape.68
  256.1 4.6 convolution_bitcast_fusion.2
  260.7 266.6 %all-reduce.8.cloned.1.call-done = (f32[147456]{0:T(1024)}, f32[589824]{0:T(1024)}, f32[589824]{0:T(1024)}) async-done(((f32[147456]{0:T(1024)}, f32[589824]{0:T(1024)}, f32[589824]{0:T(1024)}), (f32[147456]{0:T(1024)}, f32[589824]{0:T(1024)}, f32[589824]{0:T(1024)})) %all-reduce.8.cloned.1.call-update) | async-done | bytes 5308432
  527.3 1.4 dynamic-slice.1
  528.7 1.4 dynamic-slice.2
  530.1 1.4 dynamic-slice
  (69 shorter events, 41.5 us)
Async XLA Ops:
  7.2 176.8 %copy-start = (bf16[1,1,5,512,512]{4,3,2,1,0:T(8,128)(2,1)S(1)}, bf16[1,1,5,512,512]{4,3,2,1,0:T(8,128)(2,1)}, u32[]{:S(2)}) copy-start(bf16[1,1,5,512,512]{4,3,2,1,0:T(8,128)(2,1)} %param.20) | copy-start | bytes 7864324
  153.1 19.1 %copy-start.6 = (s32[1,1,5]{2,1,0:T(1,128)S(1)}, s32[1,1,5]{2,1,0:T(1,128)}, u32[]{:S(2)}) copy-start(s32[1,1,5]{2,1,0:T(1,128)} %param.21) | copy-start | bytes 64
  161.6 22.4 %all-to-all-start = ((bf16[16,32,384]{2,1,0:T(8,128)(2,1)}), bf16[16,32,384]{2,1,0:T(8,128)(2,1)}, u32[]{:S(2)}, u32[]{:S(2)}) async-start(bf16[16,32,384]{2,1,0:T(8,128)(2,1)} %fusion.15), calls=%async_computation | async-start | bytes 786432 | tf_op jit(solution)/shard_map/all_to_all | solution.py:102
  170.2 357.1 %all-reduce.8.cloned.1.call-start = ((), (), s32[]{:S(2)}) async-start(), calls=%async_computation.1 | async-start | bytes 10616832
  186.2 3.5 copy-start.1
  186.2 16.9 %copy-start.2 = (f32[16,32,1536]{2,1,0:T(8,128)S(1)}, f32[16,32,1536]{2,1,0:T(8,128)}, u32[]{:S(2)}) copy-start(f32[16,32,1536]{2,1,0:T(8,128)} %get-tuple-element.183) | copy-start | bytes 9437188
  186.2 16.9 %copy-start.4 = (f32[15,32,384]{2,1,0:T(8,128)S(1)}, f32[15,32,384]{2,1,0:T(8,128)}, u32[]{:S(2)}) copy-start(f32[15,32,384]{2,1,0:T(8,128)} %slice.80) | copy-start | bytes 2211844
  189.7 36.1 %collective-permute-start = (f32[1,512,384]{1,2,0:T(8,128)}, f32[1,512,384]{1,2,0:T(8,128)}, u32[]{:S(2)}, u32[]{:S(2)}) collective-permute-start(f32[1,512,384]{1,2,0:T(8,128)} %get-tuple-element.241), channel_id=1, source_target_pairs={{2,0},{3,1},{4,2},{5,3},{6,4},{7,5},{8,6},{9,7},{10,8},{11,9},{12,... | collective-permute-start | bytes 2359304 | tf_op jit(solution)/shard_map/ppermute | solution.py:10
  194.6 35.9 %collective-permute-start.1 = (f32[1,512,384]{1,2,0:T(8,128)}, f32[1,512,384]{1,2,0:T(8,128)}, u32[]{:S(2)}, u32[]{:S(2)}) collective-permute-start(f32[1,512,384]{1,2,0:T(8,128)} %get-tuple-element.244), channel_id=1, source_target_pairs={{1,0},{2,1},{3,2},{4,3},{5,4},{6,5},{7,6},{8,7},{9,8},{10,9},{11,1... | collective-permute-start | bytes 2359304 | tf_op jit(solution)/shard_map/ppermute | solution.py:10
  197.7 33.2 %collective-permute-start.2 = (f32[1,512,384]{1,2,0:T(8,128)}, f32[1,512,384]{1,2,0:T(8,128)}, u32[]{:S(2)}, u32[]{:S(2)}) collective-permute-start(f32[1,512,384]{1,2,0:T(8,128)} %get-tuple-element.243), channel_id=1, source_target_pairs={{0,1},{1,2},{2,3},{3,4},{4,5},{5,6},{6,7},{7,8},{8,9},{9,10},{10,1... | collective-permute-start | bytes 2359304 | tf_op jit(solution)/shard_map/ppermute | solution.py:10
  200.5 46.8 %collective-permute-start.3 = (f32[1,512,384]{1,2,0:T(8,128)}, f32[1,512,384]{1,2,0:T(8,128)}, u32[]{:S(2)}, u32[]{:S(2)}) collective-permute-start(f32[1,512,384]{1,2,0:T(8,128)} %get-tuple-element.242), channel_id=1, source_target_pairs={{0,2},{1,3},{2,4},{3,5},{4,6},{5,7},{6,8},{7,9},{8,10},{9,11},{10,... | collective-permute-start | bytes 2359304 | tf_op jit(solution)/shard_map/ppermute | solution.py:10
  208.6 3.2 copy-start.5
  225.8 24.1 %copy-start.3 = (f32[1,512,384]{2,1,0:T(8,128)S(1)}, f32[1,512,384]{2,1,0:T(8,128)}, u32[]{:S(2)}) copy-start(f32[1,512,384]{2,1,0:T(8,128)} %param.19) | copy-start | bytes 2359300
Sparse Core Ops, SparseCore 0:
  256.2 271.0 all-reduce.7
where the time goes:
time: 542 us; the launch traced here: 538 us
  waiting for transfers between devices  300 us (55%)
  matrix products  102 us (19%)
  other arithmetic  56.7 us (10%)
  local copies, waits for them, and re-layouts  43 us (8%)
  starting transfers between devices  22.1 us (4%)
  between operations  14.2 us (3%)
    unnamed x2, waiting for transfers between devices  267 us
    dot_general x16, matrix products, reverse_step(): jnp.dot(pre_grad, recur_weight.T, precision=lax.Precision.HIGHEST, prefer...  71.7 us
    mul x16, other arithmetic, reverse_step(): return ((new_rec, cell_total * forget), pre_grad)  24.4 us
    ppermute x4, waiting for transfers between devices, passed_along(): return lax.ppermute(shard, axis, pairs)  21.5 us
    squeeze x16, local copies, waits for them, and re-layouts, cell_backward(): lax.scan(reverse_step, begin, (gate_vals, cell_vals, prev_cells, out_grad...  15 us
    ppermute x4, starting transfers between devices, passed_along(): return lax.ppermute(shard, axis, pairs)  13.4 us
    mul x16, other arithmetic, reverse_step(): cell_total * candidate * in_gate * (1.0 - in_gate)  13.2 us
    all_to_all x1, waiting for transfers between devices, local(): lax.all_to_all(conv_in_grad.astype(jnp.bfloat16), 'snap', split_axis=0, c...  11.8 us
  transfers between devices with their start and end apart: 6, of which 5 were waited for; matrix products, arithmetic and copies ran while one was open for 5% of the time, Pallas kernels for 0%

commit v1 on v0

--- a/solution.py
+++ b/solution.py
@@ -99,8 +99,14 @@
         lax.psum_scatter(input_term, ("snap", "vert"), scatter_dimension=0, tiled=True),
         lax.psum_scatter(recur_term, ("snap", "vert"), scatter_dimension=0, tiled=True),
     )
-    rounded = lax.all_to_all(
-        conv_in_grad.astype(jnp.bfloat16), "snap", split_axis=0, concat_axis=1, tiled=True
+    rounded = jnp.concatenate(
+        lax.all_to_all(
+            jnp.stack(jnp.split(conv_in_grad.astype(jnp.bfloat16), lax.axis_size("snap"), axis=0)),
+            "snap",
+            0,
+            0,
+        ),
+        axis=1,
     )
     tiles = tile_values[:, 0]
     partial_value = jnp.einsum("skij,sif->skjf", tiles, rounded, preferred_element_type=jnp.float32)

time: 542 us -> 551 us (1.017)
  local copies, waits for them, and re-layouts: 43 us -> 52.8 us
    unnamed x17 -> x32, local copies, waits for them, and re-layouts: 5.98 us -> 15.1 us
where the time goes in v1:
time: 551 us; the launch traced here: 547 us
  waiting for transfers between devices  300 us (54%)
  matrix products  102 us (19%)
  other arithmetic  56.7 us (10%)
  local copies, waits for them, and re-layouts  52.8 us (10%)
  starting transfers between devices  22.2 us (4%)
  between operations  14.2 us (3%)
    unnamed x2, waiting for transfers between devices  267 us
    dot_general x16, matrix products, reverse_step(): jnp.dot(pre_grad, recur_weight.T, precision=lax.Precision.HIGHEST, prefer...  71.7 us
    mul x16, other arithmetic, reverse_step(): return ((new_rec, cell_total * forget), pre_grad)  24.4 us
    ppermute x4, waiting for transfers between devices, passed_along(): return lax.ppermute(shard, axis, pairs)  21.3 us
    unnamed x32, local copies, waits for them, and re-layouts  15.1 us
    squeeze x16, local copies, waits for them, and re-layouts, cell_backward(): lax.scan(reverse_step, begin, (gate_vals, cell_vals, prev_cells, out_grad...  15 us
    ppermute x4, starting transfers between devices, passed_along(): return lax.ppermute(shard, axis, pairs)  13.6 us
    mul x16, other arithmetic, reverse_step(): cell_total * candidate * in_gate * (1.0 - in_gate)  13.2 us
  transfers between devices with their start and end apart: 6, of which 5 were waited for; matrix products, arithmetic and copies ran while one was open for 5% of the time, Pallas kernels for 0%

profile of v1, /device:TPU:8, one launch (start us, length us, event | category | flops | bytes accessed | tf_op | source)
XLA Modules:
  0.0 547.4 jit_solution(3144443936734232795)
XLA Ops:
  7.2 1.2 slice.74
  8.4 2.0 convert_element_type.19
  10.4 3.5 convert_element_type.18
  14.8 2.1 broadcast_in_dim.15
  17.5 135.6 %while.19 = (s32[]{:T(128)}, f32[32,384]{1,0:T(8,128)}, f32[32,384]{1,0:T(8,128)}, f32[16,32,1536]{2,1,0:T(8,128)}, f32[16,32,384]{2,1,0:T(8,128)}, /*index=5*/f...) while((s32[]{:T(128)}, f32[32,384]{1,0:T(8,128)}, ...), condition=%wide.region_1.2_spmd.clone, body=%wide.region_0.1_spmd.clone.sunk | while | flops 227082240 | bytes 4227227 | solution.py:51
  18.4 1.5 slice_multiply_fusion.2
  21.5 4.5 fusion.44
  26.9 1.5 slice_multiply_fusion.2
  29.9 4.5 fusion.44
  35.4 1.5 slice_multiply_fusion.2
  38.4 4.5 fusion.44
  43.8 1.5 slice_multiply_fusion.2
  46.9 4.5 fusion.44
  52.3 1.5 slice_multiply_fusion.2
  55.3 4.5 fusion.44
  60.8 1.5 slice_multiply_fusion.2
  63.8 4.5 fusion.44
  69.2 1.5 slice_multiply_fusion.2
  72.3 4.5 fusion.44
  77.7 1.5 slice_multiply_fusion.2
  80.8 4.5 fusion.44
  86.2 1.5 slice_multiply_fusion.2
  89.3 4.5 fusion.44
  94.7 1.5 slice_multiply_fusion.2
  97.8 4.5 fusion.44
  103.2 1.5 slice_multiply_fusion.2
  106.2 4.5 fusion.44
  111.7 1.5 slice_multiply_fusion.2
  114.7 4.5 fusion.44
  120.2 1.5 slice_multiply_fusion.2
  123.2 4.5 fusion.44
  128.6 1.5 slice_multiply_fusion.2
  131.7 4.5 fusion.44
  137.1 1.5 slice_multiply_fusion.2
  140.2 4.5 fusion.44
  145.6 1.5 slice_multiply_fusion.2
  148.6 4.5 fusion.44
  153.1 7.8 %fusion.15 = bf16[16,32,384]{2,1,0:T(8,128)(2,1)S(1)} fusion(f32[16,32,1536]{2,1,0:T(8,128)} %get-tuple-element.183, f32[384,1536]{1,0:T(8,128)} %param.16), kind=kOutput, calls=%fused_computation.28 | convolution fusion | flops 3624075264 | bytes 5898240 | tf_op jit(solution)/shard_map/tvg,fg->tvf/dot_general | solution.py:77
  170.7 8.6 %all-to-all-start = ((bf16[16,1,32,384]{3,2,1,0:T(8,128)(2,1)}), bf16[16,1,32,384]{3,2,1,0:T(8,128)(2,1)}, u32[]{:S(2)}, u32[]{:S(2)}) async-start(bf16[16,1,32,384]{3,2,1,0:T(8,128)(2,1)} %constant_dynamic-update-slice_fusion), calls=%async_computation | async-start | bytes 786432 | tf_op jit(solution)/shard_map/all_to_all | solution.py:103
  179.3 1.9 slice.80
  181.3 11.8 %all-to-all-done = bf16[16,1,32,384]{3,2,1,0:T(8,128)(2,1)} async-done(((bf16[16,1,32,384]{3,2,1,0:T(8,128)(2,1)}), bf16[16,1,32,384]{3,2,1,0:T(8,128)(2,1)}, u32[]{:S(2)}, u32[]{:S(2)}) %all-to-all-start) | async-done | bytes 393248 | tf_op jit(solution)/shard_map/all_to_all | solution.py:103
  193.0 2.2 multiply_bitcast_fusion
  195.3 1.7 slice_bitcast_fusion.3
  197.0 1.8 copy-done.1
  198.8 4.9 collective-permute-start
  203.7 3.1 collective-permute-start.1
  206.8 2.8 collective-permute-start.2
  209.6 2.8 collective-permute-start.3
  212.4 5.4 convolution_bitcast_fusion
  217.8 3.2 reshape.68
  221.0 7.7 %convolution_bitcast_fusion.1 = f32[384,1536]{0,1:T(8,128)} fusion(f32[16,32,1536]{2,1,0:T(8,128)} %get-tuple-element.183, f32[16,32,384]{2,1,0:T(8,128)S(1)} %copy-done.5), kind=kOutput, calls=%fused_computation.22 | convolution fusion | flops 3623878656 | bytes 6291456 | tf_op jit(solution)/shard_map/tvf,tvg->fg/dot_general | solution.py:84
  228.7 3.1 copy.20
  231.9 3.1 reshape.67
  235.0 4.6 collective-permute-done.1
  240.0 16.3 %collective-permute-done.3 = f32[1,512,384]{1,2,0:T(8,128)} collective-permute-done((f32[1,512,384]{1,2,0:T(8,128)}, f32[1,512,384]{1,2,0:T(8,128)}, u32[]{:S(2)}, u32[]{:S(2)}) %collective-permute-start.3) | collective-permute-done | bytes 786464 | tf_op jit(solution)/shard_map/ppermute | solution.py:10
  256.4 2.5 fusion.22
  258.9 2.2 convolution_bitcast_fusion.3
  261.1 2.1 copy.19
  263.2 1.9 reshape.66
  265.2 4.6 convolution_bitcast_fusion.2
  269.8 266.6 %all-reduce.8.cloned.1.call-done = (f32[147456]{0:T(1024)}, f32[589824]{0:T(1024)}, f32[589824]{0:T(1024)}) async-done(((f32[147456]{0:T(1024)}, f32[589824]{0:T(1024)}, f32[589824]{0:T(1024)}), (f32[147456]{0:T(1024)}, f32[589824]{0:T(1024)}, f32[589824]{0:T(1024)})) %all-reduce.8.cloned.1.call-update) | async-done | bytes 5308432
  536.4 1.4 dynamic-slice.1
  537.8 1.4 dynamic-slice.2
  539.2 1.4 dynamic-slice
  (85 shorter events, 51.3 us)
Async XLA Ops:
  7.2 185.9 %copy-start = (bf16[1,1,5,512,512]{4,3,2,1,0:T(8,128)(2,1)S(1)}, bf16[1,1,5,512,512]{4,3,2,1,0:T(8,128)(2,1)}, u32[]{:S(2)}) copy-start(bf16[1,1,5,512,512]{4,3,2,1,0:T(8,128)(2,1)} %param.20) | copy-start | bytes 7864324
  153.1 28.2 %copy-start.6 = (s32[1,1,5]{2,1,0:T(1,128)S(1)}, s32[1,1,5]{2,1,0:T(1,128)}, u32[]{:S(2)}) copy-start(s32[1,1,5]{2,1,0:T(1,128)} %param.21) | copy-start | bytes 64
  170.7 22.4 %all-to-all-start = ((bf16[16,1,32,384]{3,2,1,0:T(8,128)(2,1)}), bf16[16,1,32,384]{3,2,1,0:T(8,128)(2,1)}, u32[]{:S(2)}, u32[]{:S(2)}) async-start(bf16[16,1,32,384]{3,2,1,0:T(8,128)(2,1)} %constant_dynamic-update-slice_fusion), calls=%async_computation | async-start | bytes 786432 | tf_op jit(solution)/shard_map/all_to_all | solution.py:103
  179.3 357.1 %all-reduce.8.cloned.1.call-start = ((), (), s32[]{:S(2)}) async-start(), calls=%async_computation.1 | async-start | bytes 10616832
  195.2 3.5 copy-start.1
  195.3 17.1 %copy-start.2 = (f32[16,32,1536]{2,1,0:T(8,128)S(1)}, f32[16,32,1536]{2,1,0:T(8,128)}, u32[]{:S(2)}) copy-start(f32[16,32,1536]{2,1,0:T(8,128)} %get-tuple-element.183) | copy-start | bytes 9437188
  195.3 17.1 %copy-start.4 = (f32[15,32,384]{2,1,0:T(8,128)S(1)}, f32[15,32,384]{2,1,0:T(8,128)}, u32[]{:S(2)}) copy-start(f32[15,32,384]{2,1,0:T(8,128)} %slice.80) | copy-start | bytes 2211844
  198.8 36.2 %collective-permute-start = (f32[1,512,384]{1,2,0:T(8,128)}, f32[1,512,384]{1,2,0:T(8,128)}, u32[]{:S(2)}, u32[]{:S(2)}) collective-permute-start(f32[1,512,384]{1,2,0:T(8,128)} %get-tuple-element.241), channel_id=1, source_target_pairs={{2,0},{3,1},{4,2},{5,3},{6,4},{7,5},{8,6},{9,7},{10,8},{11,9},{12,... | collective-permute-start | bytes 2359304 | tf_op jit(solution)/shard_map/ppermute | solution.py:10
  203.7 35.9 %collective-permute-start.1 = (f32[1,512,384]{1,2,0:T(8,128)}, f32[1,512,384]{1,2,0:T(8,128)}, u32[]{:S(2)}, u32[]{:S(2)}) collective-permute-start(f32[1,512,384]{1,2,0:T(8,128)} %get-tuple-element.244), channel_id=1, source_target_pairs={{1,0},{2,1},{3,2},{4,3},{5,4},{6,5},{7,6},{8,7},{9,8},{10,9},{11,1... | collective-permute-start | bytes 2359304 | tf_op jit(solution)/shard_map/ppermute | solution.py:10
  206.8 33.2 %collective-permute-start.2 = (f32[1,512,384]{1,2,0:T(8,128)}, f32[1,512,384]{1,2,0:T(8,128)}, u32[]{:S(2)}, u32[]{:S(2)}) collective-permute-start(f32[1,512,384]{1,2,0:T(8,128)} %get-tuple-element.243), channel_id=1, source_target_pairs={{0,1},{1,2},{2,3},{3,4},{4,5},{5,6},{6,7},{7,8},{8,9},{9,10},{10,1... | collective-permute-start | bytes 2359304 | tf_op jit(solution)/shard_map/ppermute | solution.py:10
  209.6 46.8 %collective-permute-start.3 = (f32[1,512,384]{1,2,0:T(8,128)}, f32[1,512,384]{1,2,0:T(8,128)}, u32[]{:S(2)}, u32[]{:S(2)}) collective-permute-start(f32[1,512,384]{1,2,0:T(8,128)} %get-tuple-element.242), channel_id=1, source_target_pairs={{0,2},{1,3},{2,4},{3,5},{4,6},{5,7},{6,8},{7,9},{8,10},{9,11},{10,... | collective-permute-start | bytes 2359304 | tf_op jit(solution)/shard_map/ppermute | solution.py:10
  217.8 3.2 copy-start.5
  235.0 23.9 %copy-start.3 = (f32[1,512,384]{2,1,0:T(8,128)S(1)}, f32[1,512,384]{2,1,0:T(8,128)}, u32[]{:S(2)}) copy-start(f32[1,512,384]{2,1,0:T(8,128)} %param.19) | copy-start | bytes 2359300
Sparse Core Ops, SparseCore 0:
  265.3 271.0 all-reduce.7
